TPU v7x, 32 devices: a whole 2x2x4 slice. The times are simulated.
32 devices in a mesh: groups: 2 (over x), ta: 4 (over y, core), xy: 4 (over z).
Axes of the slice: x: 2, y: 2, z: 4, core: 2. Of those that a mesh axis runs over, the one named last changes fastest.
Arguments:
- sources: bfloat16 [8, 4, 4, 8, 96, 256], P('groups', 'ta', 'xy'), parts along dimension 0, may hold values from -24 to 24
- coarse_links: bfloat16 [18, 4, 4, 4, 8, 96, 96], P('groups', None, 'ta', 'xy'), parts along dimension 0, may hold values from -0.119628906 to 0.119628906
Outputs:
- solution: float32 [8, 4, 4, 8, 96, 256], P('groups', 'ta', 'xy'), parts along dimension 0
There are 2 independent parts, one for each index of `groups`. A program takes and returns all parts, laid end to end along the dimension named above; each array names one. Nothing has to cross between parts.
All inputs are finite; a program needn't handle non-finite values.
Results may differ from a plain program's by a relative error of at most 0.0019.
The roundings to bfloat16 on the way count: a program that leaves them out, or rounds other values in their place, can miss the bound.
Values may be sent and summed in bfloat16 or wider, within the bound.
A program may use at most 128 MiB of HBM per device.

v0:
```python
import jax
import jax.numpy as jnp
from jax import lax
from jax.sharding import PartitionSpec as P

ITERS = 2
mass_term = 2.0


def with_halo(cells, sides, width):
    for axis, dim in sides:
        count = lax.axis_size(axis)
        head = lax.slice_in_dim(cells, 0, width, axis=dim)
        tail = lax.slice_in_dim(cells, cells.shape[dim] - width, cells.shape[dim], axis=dim)
        cells = jnp.concatenate(
            [
                lax.ppermute(tail, axis, [(i, (i + 1) % count) for i in range(count)]),
                cells,
                lax.ppermute(head, axis, [((i + 1) % count, i) for i in range(count)]),
            ],
            axis=dim,
        )
    return cells


def link_product(link_field, vector, flipped):
    einsum_form = "abcdio,abcdir->abcdor" if flipped else "abcdoi,abcdir->abcdor"
    return jnp.einsum(einsum_form, link_field, vector, preferred_element_type=jnp.float32)


def widen(vector):
    return with_halo(vector, (("ta", 1), ("xy", 2)), 1)


def apply_forward(rounded, coarse_links):
    padded = widen(rounded)
    neighbours = (
        padded[:, 2:, 1:-1],
        padded[:, :-2, 1:-1],
        padded[:, 1:-1, 2:],
        padded[:, 1:-1, :-2],
        jnp.roll(rounded, -1, 0),
        jnp.roll(rounded, 1, 0),
        jnp.roll(rounded, -1, 3),
        jnp.roll(rounded, 1, 3),
    )
    summed = mass_term * rounded.astype(jnp.float32) + link_product(coarse_links[0], rounded, False)
    for number in range(8):
        summed = summed + link_product(coarse_links[number + 1], neighbours[number], False)
    return summed


def local_adjoint(image_vec, coarse_links):
    summed = mass_term * image_vec.astype(jnp.float32) + link_product(
        coarse_links[0], image_vec, True
    )
    plane_moves = ((4, 1, 0), (5, -1, 0), (6, 1, 3), (7, -1, 3))
    for number, sign_value, axis_number in plane_moves:
        adjoint_term = link_product(coarse_links[number + 1], image_vec, True).astype(jnp.bfloat16)
        summed = summed + jnp.roll(adjoint_term, sign_value, axis_number).astype(jnp.float32)
    return summed


def adjoint_products(image_vec, coarse_links):
    summed = local_adjoint(image_vec, coarse_links)
    adjoint_terms = [
        link_product(coarse_links[number + 1], image_vec, True).astype(jnp.bfloat16)
        for number in range(4)
    ]
    rim_time = jnp.concatenate((adjoint_terms[1], adjoint_terms[0]), axis=1)
    ext_time = with_halo(rim_time, (("ta", 1),), 1)
    rim_space = jnp.concatenate((adjoint_terms[3], adjoint_terms[2]), axis=2)
    ext_space = with_halo(rim_space, (("xy", 2),), 1)
    shifted = (
        jnp.concatenate((ext_time[:, :1], adjoint_terms[0][:, :-1]), axis=1),
        jnp.concatenate((adjoint_terms[1][:, 1:], ext_time[:, -1:]), axis=1),
        jnp.concatenate((ext_space[:, :, :1], adjoint_terms[2][:, :, :-1]), axis=2),
        jnp.concatenate((adjoint_terms[3][:, :, 1:], ext_space[:, :, -1:]), axis=2),
    )
    for moved_term in shifted:
        summed = summed + moved_term.astype(jnp.float32)
    return summed


def gram(left_vec, right_vec):
    left_rows = left_vec.reshape((-1,) + left_vec.shape[-2:])
    right_rows = right_vec.reshape((-1,) + right_vec.shape[-2:])
    return jnp.einsum("sir,sit->rt", left_rows, right_rows, precision=lax.Precision.HIGHEST)


def combine(vector, coefficients):
    return jnp.einsum("abcdir,rt->abcdit", vector, coefficients, precision=lax.Precision.HIGHEST)


def solve_spd(matrix, right_side):
    factor = jnp.linalg.cholesky(matrix)
    return jax.scipy.linalg.cho_solve((factor, True), right_side)


def residual_norms(residual):
    return lax.psum(gram(residual, residual), ("ta", "xy"))


def body(sources, coarse_links):
    residual = sources.astype(jnp.float32)
    solution = jnp.zeros_like(residual)
    search = residual
    energy = residual_norms(residual)
    for iteration in range(ITERS):
        rounded = search.astype(jnp.bfloat16)
        image_vec = apply_forward(rounded, coarse_links).astype(jnp.bfloat16)
        normal_image = adjoint_products(image_vec, coarse_links)
        curvature, cross_term, image_gram = lax.psum(
            (
                gram(search, normal_image),
                gram(residual, normal_image),
                gram(normal_image, normal_image),
            ),
            ("ta", "xy"),
        )
        alpha_step = solve_spd(curvature, energy)
        solution = solution + combine(search, alpha_step)
        if iteration + 1 < ITERS:
            residual = residual - combine(normal_image, alpha_step)
            mixed_term = jnp.dot(cross_term, alpha_step, precision=lax.Precision.HIGHEST)
            quadratic = jnp.dot(
                alpha_step.T,
                jnp.dot(image_gram, alpha_step, precision=lax.Precision.HIGHEST),
                precision=lax.Precision.HIGHEST,
            )
            fresh_energy = energy - mixed_term - mixed_term.T + quadratic
            beta_step = solve_spd(energy, fresh_energy)
            search = residual + combine(search, beta_step)
            energy = fresh_energy
    return solution


def solution(mesh):
    return jax.shard_map(
        body,
        mesh=mesh,
        in_specs=(
            P("groups", "ta", "xy", None, None, None),
            P("groups", None, "ta", "xy", None, None, None),
        ),
        out_specs=P("groups", "ta", "xy", None, None, None),
        check_vma=False,
    )
```

profile of v0, /device:TPU:0, one launch (start us, length us, event | category | flops | bytes accessed | tf_op | source)
XLA Modules:
  0.0 1095.6 jit_solution(8653942792856709858)
XLA Ops:
  9.0 35.1 %collective-permute-done = bf16[4,1,1,8,96,256]{5,4,3,0,2,1:T(8,128)(2,1)S(1)} collective-permute-done((bf16[4,1,1,8,96,256]{5,4,3,0,2,1:T(8,128)(2,1)}, bf16[4,1,1,8,96,256]{5,4,3,0,2,1:T(8,128)(2,1)S(1)}, u32[]{:S(2)}, u32[]{:S(2)}) %collective-permute-start) | collective-permute-done | bytes 1572896 | tf_op jit(solution)/shard_map/ppermute | solution.py:19
  65.1 87.6 %collective-permute-done.2 = bf16[4,3,1,8,96,256]{5,4,3,0,2,1:T(8,128)(2,1)S(1)} collective-permute-done((bf16[4,3,1,8,96,256]{5,4,3,0,2,1:T(8,128)(2,1)S(1)}, bf16[4,3,1,8,96,256]{5,4,3,0,2,1:T(8,128)(2,1)S(1)}, u32[]{:S(2)}, u32[]{:S(2)}) %collective-permute-start.2) | collective-permute-done | bytes 4718624 | tf_op jit(solution)/shard_map/ppermute | solution.py:19
  155.1 98.2 %collective-permute-done.3 = bf16[4,3,1,8,96,256]{5,4,3,0,2,1:T(8,128)(2,1)} collective-permute-done((bf16[4,3,1,8,96,256]{5,4,3,0,2,1:T(8,128)(2,1)S(1)}, bf16[4,3,1,8,96,256]{5,4,3,0,2,1:T(8,128)(2,1)}, u32[]{:S(2)}, u32[]{:S(2)}) %collective-permute-start.3) | collective-permute-done | bytes 4718624 | tf_op jit(solution)/shard_map/ppermute | solution.py:17
  274.3 24.5 %collective-permute-done.4 = bf16[4,1,1,8,96,256]{5,4,3,0,2,1:T(8,128)(2,1)S(1)} collective-permute-done((bf16[4,1,1,8,96,256]{5,4,3,0,2,1:T(8,128)(2,1)S(1)}, bf16[4,1,1,8,96,256]{5,4,3,0,2,1:T(8,128)(2,1)S(1)}, u32[]{:S(2)}, u32[]{:S(2)}) %collective-permute-start.4) | collective-permute-done | bytes 1572896 | tf_op jit(solution)/shard_map/ppermute | solution.py:17
  305.4 33.0 %collective-permute-done.7 = bf16[4,1,1,8,96,256]{5,4,3,0,2,1:T(8,128)(2,1)S(1)} collective-permute-done((bf16[4,1,1,8,96,256]{5,4,3,0,2,1:T(8,128)(2,1)S(1)}, bf16[4,1,1,8,96,256]{5,4,3,0,2,1:T(8,128)(2,1)S(1)}, u32[]{:S(2)}, u32[]{:S(2)}) %collective-permute-start.7) | collective-permute-done | bytes 1572896 | tf_op jit(solution)/shard_map/ppermute | solution.py:19
  350.7 91.8 %all-reduce.7.cloned.1.call-done = (f32[256,256]{0,1:T(8,128)}, f32[256,256]{0,1:T(8,128)}, f32[256,256]{1,0:T(8,128)}) async-done(((f32[256,256]{0,1:T(8,128)}, f32[256,256]{0,1:T(8,128)}, f32[256,256]{1,0:T(8,128)}), (f32[256,256]{0,1:T(8,128)}, f32[256,256]{0,1:T(8,128)}, f32[256,256]{1,0:T(8,128)})) %all-reduce.7.cloned.1.call-update) | async-done | bytes 786448 | tf_op jit(solution)/shard_map/psum | solution.py:101
  444.7 11.7 %cholesky.206 = f32[128,128]{1,0:T(8,128)S(1)} custom-call(f32[128,128]{1,0:T(8,128)S(1)} %cholesky.273), custom_call_target="Cholesky" | custom-call | tf_op jit(solution)/shard_map/jit(cholesky)/cholesky | solution.py:96
  456.5 9.8 custom-call.19
  466.8 11.7 %cholesky.223 = f32[128,128]{1,0:T(8,128)S(1)} custom-call(f32[128,128]{1,0:T(8,128)S(1)} %convolution_subtract_fusion.7), custom_call_target="Cholesky" | custom-call | tf_op jit(solution)/shard_map/jit(cholesky)/cholesky | solution.py:96
  485.6 19.7 %custom-call.20 = f32[2,128,128]{1,2,0:T(8,128)S(1)} custom-call(f32[2,128,128]{2,1,0:T(8,128)S(1)} %get-tuple-element.28), custom_call_target="InvertDiagBlocksLowerTriangular" | custom-call | tf_op jit(solution)/shard_map/jit(_cho_solve)/triangular_solve | solution.py:97
  505.5 11.7 %cholesky.172 = f32[128,128]{1,0:T(8,128)S(1)} custom-call(f32[128,128]{1,0:T(8,128)S(1)} %cholesky.270), custom_call_target="Cholesky" | custom-call | tf_op jit(solution)/shard_map/jit(cholesky)/cholesky | solution.py:96
  517.3 9.8 custom-call.17
  527.6 11.7 %cholesky.189 = f32[128,128]{1,0:T(8,128)S(1)} custom-call(f32[128,128]{1,0:T(8,128)S(1)} %convolution_subtract_fusion.8), custom_call_target="Cholesky" | custom-call | tf_op jit(solution)/shard_map/jit(cholesky)/cholesky | solution.py:96
  545.8 20.1 %custom-call.18 = f32[2,128,128]{1,2,0:T(8,128)S(1)} custom-call(f32[2,128,128]{2,1,0:T(8,128)S(1)} %get-tuple-element.27), custom_call_target="InvertDiagBlocksLowerTriangular" | custom-call | tf_op jit(solution)/shard_map/jit(_cho_solve)/triangular_solve | solution.py:97
  577.7 33.4 %collective-permute-done.8 = bf16[4,1,1,8,96,256]{5,4,3,0,2,1:T(8,128)(2,1)S(1)} collective-permute-done((bf16[4,1,1,8,96,256]{5,4,3,0,2,1:T(8,128)(2,1)S(1)}, bf16[4,1,1,8,96,256]{5,4,3,0,2,1:T(8,128)(2,1)S(1)}, u32[]{:S(2)}, u32[]{:S(2)}) %collective-permute-start.8) | collective-permute-done | bytes 1572896 | tf_op jit(solution)/shard_map/ppermute | solution.py:19
  631.5 86.8 %collective-permute-done.10 = bf16[4,3,1,8,96,256]{5,4,3,0,2,1:T(8,128)(2,1)S(1)} collective-permute-done((bf16[4,3,1,8,96,256]{5,4,3,0,2,1:T(8,128)(2,1)S(1)}, bf16[4,3,1,8,96,256]{5,4,3,0,2,1:T(8,128)(2,1)S(1)}, u32[]{:S(2)}, u32[]{:S(2)}) %collective-permute-start.10) | collective-permute-done | bytes 4718624 | tf_op jit(solution)/shard_map/ppermute | solution.py:19
  720.6 99.8 %collective-permute-done.11 = bf16[4,3,1,8,96,256]{5,4,3,0,2,1:T(8,128)(2,1)} collective-permute-done((bf16[4,3,1,8,96,256]{5,4,3,0,2,1:T(8,128)(2,1)S(1)}, bf16[4,3,1,8,96,256]{5,4,3,0,2,1:T(8,128)(2,1)}, u32[]{:S(2)}, u32[]{:S(2)}) %collective-permute-start.11) | collective-permute-done | bytes 4718624 | tf_op jit(solution)/shard_map/ppermute | solution.py:17
  842.0 29.1 %collective-permute-done.12 = bf16[4,1,1,8,96,256]{5,4,3,0,2,1:T(8,128)(2,1)S(1)} collective-permute-done((bf16[4,1,1,8,96,256]{5,4,3,0,2,1:T(8,128)(2,1)S(1)}, bf16[4,1,1,8,96,256]{5,4,3,0,2,1:T(8,128)(2,1)S(1)}, u32[]{:S(2)}, u32[]{:S(2)}) %collective-permute-start.12) | collective-permute-done | bytes 1572896 | tf_op jit(solution)/shard_map/ppermute | solution.py:17
  876.9 30.4 %collective-permute-done.15 = bf16[4,1,1,8,96,256]{5,4,3,0,2,1:T(8,128)(2,1)} collective-permute-done((bf16[4,1,1,8,96,256]{5,4,3,0,2,1:T(8,128)(2,1)S(1)}, bf16[4,1,1,8,96,256]{5,4,3,0,2,1:T(8,128)(2,1)}, u32[]{:S(2)}, u32[]{:S(2)}) %collective-permute-start.15) | collective-permute-done | bytes 1572896 | tf_op jit(solution)/shard_map/ppermute | solution.py:19
  921.1 86.1 %all-reduce.5.cloned.1.call-done = f32[256,256]{0,1:T(8,128)} async-done(((f32[256,256]{0,1:T(8,128)}), f32[256,256]{0,1:T(8,128)}) %all-reduce.5.cloned.1.call-update) | async-done | bytes 262160 | tf_op jit(solution)/shard_map/psum | solution.py:113
  1010.8 11.7 %cholesky.240 = f32[128,128]{1,0:T(8,128)S(1)} custom-call(f32[128,128]{1,0:T(8,128)S(1)} %cholesky.276), custom_call_target="Cholesky" | custom-call | tf_op jit(solution)/shard_map/jit(cholesky)/cholesky | solution.py:96
  1023.3 10.0 custom-call.21
  1036.1 11.7 %cholesky.257 = f32[128,128]{1,0:T(8,128)S(1)} custom-call(f32[128,128]{1,0:T(8,128)S(1)} %convolution_subtract_fusion.6), custom_call_target="Cholesky" | custom-call | tf_op jit(solution)/shard_map/jit(cholesky)/cholesky | solution.py:96
  1058.8 20.5 %custom-call.22 = f32[2,128,128]{1,2,0:T(8,128)S(1)} custom-call(f32[2,128,128]{2,1,0:T(8,128)} %copy-done.13), custom_call_target="InvertDiagBlocksLowerTriangular" | custom-call | tf_op jit(solution)/shard_map/jit(_cho_solve)/triangular_solve | solution.py:97
  (225 shorter events, 194.4 us)
Async XLA Ops:
  6.5 436.0 %all-reduce.7.cloned.1.call-start = ((), (), s32[]{:S(2)}) async-start(), calls=%async_computation.1 | async-start | bytes 1572864 | tf_op jit(solution)/shard_map/psum | solution.py:101
  6.5 37.5 %collective-permute-start = (bf16[4,1,1,8,96,256]{5,4,3,0,2,1:T(8,128)(2,1)}, bf16[4,1,1,8,96,256]{5,4,3,0,2,1:T(8,128)(2,1)S(1)}, u32[]{:S(2)}, u32[]{:S(2)}) collective-permute-start(bf16[4,1,1,8,96,256]{5,4,3,0,2,1:T(8,128)(2,1)} %bitcast.587), channel_id=1, source_target_pairs={{4,0},{8,4},{12,8},{0,12},{5,1},{9,5},{13,9},{1,13},{6,2},{10,6},{... | collective-permute-start | bytes 4718600 | tf_op jit(solution)/shard_map/ppermute | solution.py:19
  9.0 36.1 %collective-permute-start.1 = (bf16[4,1,1,8,96,256]{5,4,3,0,2,1:T(8,128)(2,1)}, bf16[4,1,1,8,96,256]{5,4,3,0,2,1:T(8,128)(2,1)S(1)}, u32[]{:S(2)}, u32[]{:S(2)}) collective-permute-start(bf16[4,1,1,8,96,256]{5,4,3,0,2,1:T(8,128)(2,1)} %bitcast.588), channel_id=1, source_target_pairs={{0,4},{4,8},{8,12},{12,0},{1,5},{5,9},{9,13},{13,1},{2,6},{6,10},{... | collective-permute-start | bytes 4718600 | tf_op jit(solution)/shard_map/ppermute | solution.py:17
  46.9 105.9 %collective-permute-start.2 = (bf16[4,3,1,8,96,256]{5,4,3,0,2,1:T(8,128)(2,1)S(1)}, bf16[4,3,1,8,96,256]{5,4,3,0,2,1:T(8,128)(2,1)S(1)}, u32[]{:S(2)}, u32[]{:S(2)}) collective-permute-start(bf16[4,3,1,8,96,256]{5,4,3,0,2,1:T(8,128)(2,1)S(1)} %pad_maximum_fusion), channel_id=1, source_target_pairs={{1,0},{2,1},{3,2},{0,3},{5,4},{6,5},{7,6},{4,7},{9,8},{10,9},{11,1... | collective-permute-start | bytes 14155784 | tf_op jit(solution)/shard_map/ppermute | solution.py:19
  50.6 202.7 %collective-permute-start.3 = (bf16[4,3,1,8,96,256]{5,4,3,0,2,1:T(8,128)(2,1)S(1)}, bf16[4,3,1,8,96,256]{5,4,3,0,2,1:T(8,128)(2,1)}, u32[]{:S(2)}, u32[]{:S(2)}) collective-permute-start(bf16[4,3,1,8,96,256]{5,4,3,0,2,1:T(8,128)(2,1)S(1)} %pad_maximum_fusion), channel_id=1, source_target_pairs={{0,1},{1,2},{2,3},{3,0},{4,5},{5,6},{6,7},{7,4},{8,9},{9,10},{10,1... | collective-permute-start | bytes 14155784 | tf_op jit(solution)/shard_map/ppermute | solution.py:17
  264.5 34.3 %collective-permute-start.4 = (bf16[4,1,1,8,96,256]{5,4,3,0,2,1:T(8,128)(2,1)S(1)}, bf16[4,1,1,8,96,256]{5,4,3,0,2,1:T(8,128)(2,1)S(1)}, u32[]{:S(2)}, u32[]{:S(2)}) collective-permute-start(bf16[4,1,1,8,96,256]{5,4,3,0,2,1:T(8,128)(2,1)S(1)} %fusion.109), channel_id=1, source_target_pairs={{0,4},{4,8},{8,12},{12,0},{1,5},{5,9},{9,13},{13,1},{2,6},{6,10},{... | collective-permute-start | bytes 4718600 | tf_op jit(solution)/shard_map/ppermute | solution.py:17
  264.6 36.4 %collective-permute-start.5 = (bf16[4,1,1,8,96,256]{5,4,3,0,2,1:T(8,128)(2,1)S(1)}, bf16[4,1,1,8,96,256]{5,4,3,0,2,1:T(8,128)(2,1)S(1)}, u32[]{:S(2)}, u32[]{:S(2)}) collective-permute-start(bf16[4,1,1,8,96,256]{5,4,3,0,2,1:T(8,128)(2,1)S(1)} %fusion.112), channel_id=1, source_target_pairs={{4,0},{8,4},{12,8},{0,12},{5,1},{9,5},{13,9},{1,13},{6,2},{10,6},{... | collective-permute-start | bytes 4718600 | tf_op jit(solution)/shard_map/ppermute | solution.py:19
  266.3 39.1 %collective-permute-start.6 = (bf16[4,1,1,8,96,256]{5,4,3,0,2,1:T(8,128)(2,1)S(1)}, bf16[4,1,1,8,96,256]{5,4,3,0,2,1:T(8,128)(2,1)S(1)}, u32[]{:S(2)}, u32[]{:S(2)}) collective-permute-start(bf16[4,1,1,8,96,256]{5,4,3,0,2,1:T(8,128)(2,1)S(1)} %fusion.115), channel_id=1, source_target_pairs={{0,1},{1,2},{2,3},{3,0},{4,5},{5,6},{6,7},{7,4},{8,9},{9,10},{10,1... | collective-permute-start | bytes 4718600 | tf_op jit(solution)/shard_map/ppermute | solution.py:17
  267.9 70.5 %collective-permute-start.7 = (bf16[4,1,1,8,96,256]{5,4,3,0,2,1:T(8,128)(2,1)S(1)}, bf16[4,1,1,8,96,256]{5,4,3,0,2,1:T(8,128)(2,1)S(1)}, u32[]{:S(2)}, u32[]{:S(2)}) collective-permute-start(bf16[4,1,1,8,96,256]{5,4,3,0,2,1:T(8,128)(2,1)S(1)} %fusion.118), channel_id=1, source_target_pairs={{1,0},{2,1},{3,2},{0,3},{5,4},{6,5},{7,6},{4,7},{9,8},{10,9},{11,1... | collective-permute-start | bytes 4718600 | tf_op jit(solution)/shard_map/ppermute | solution.py:19
  350.7 656.6 %all-reduce.5.cloned.1.call-start = ((), (), s32[]{:S(2)}) async-start(), calls=%async_computation | async-start | bytes 524288 | tf_op jit(solution)/shard_map/psum | solution.py:113
  456.5 109.5 %copy-start.9 = (f32[256,256]{0,1:T(8,128)S(1)}, f32[256,256]{0,1:T(8,128)}, u32[]{:S(2)}) copy-start(f32[256,256]{0,1:T(8,128)} %get-tuple-element.54) | copy-start | bytes 786436
  577.2 33.9 %collective-permute-start.8 = (bf16[4,1,1,8,96,256]{5,4,3,0,2,1:T(8,128)(2,1)S(1)}, bf16[4,1,1,8,96,256]{5,4,3,0,2,1:T(8,128)(2,1)S(1)}, u32[]{:S(2)}, u32[]{:S(2)}) collective-permute-start(bf16[4,1,1,8,96,256]{5,4,3,0,2,1:T(8,128)(2,1)S(1)} %get-tuple-element.95), channel_id=1, source_target_pairs={{4,0},{8,4},{12,8},{0,12},{5,1},{9,5},{13,9},{1,13},{6,2},{10,6},{... | collective-permute-start | bytes 4718600 | tf_op jit(solution)/shard_map/ppermute | solution.py:19
  577.2 36.7 %collective-permute-start.9 = (bf16[4,1,1,8,96,256]{5,4,3,0,2,1:T(8,128)(2,1)S(1)}, bf16[4,1,1,8,96,256]{5,4,3,0,2,1:T(8,128)(2,1)S(1)}, u32[]{:S(2)}, u32[]{:S(2)}) collective-permute-start(bf16[4,1,1,8,96,256]{5,4,3,0,2,1:T(8,128)(2,1)S(1)} %get-tuple-element.95), channel_id=1, source_target_pairs={{0,4},{4,8},{8,12},{12,0},{1,5},{5,9},{9,13},{13,1},{2,6},{6,10},{... | collective-permute-start | bytes 4718600 | tf_op jit(solution)/shard_map/ppermute | solution.py:17
  614.4 103.9 %collective-permute-start.10 = (bf16[4,3,1,8,96,256]{5,4,3,0,2,1:T(8,128)(2,1)S(1)}, bf16[4,3,1,8,96,256]{5,4,3,0,2,1:T(8,128)(2,1)S(1)}, u32[]{:S(2)}, u32[]{:S(2)}) collective-permute-start(bf16[4,3,1,8,96,256]{5,4,3,0,2,1:T(8,128)(2,1)S(1)} %pad_maximum_fusion.1), channel_id=1, source_target_pairs={{1,0},{2,1},{3,2},{0,3},{5,4},{6,5},{7,6},{4,7},{9,8},{10,9},{11,1... | collective-permute-start | bytes 14155784 | tf_op jit(solution)/shard_map/ppermute | solution.py:19
  615.8 204.5 %collective-permute-start.11 = (bf16[4,3,1,8,96,256]{5,4,3,0,2,1:T(8,128)(2,1)S(1)}, bf16[4,3,1,8,96,256]{5,4,3,0,2,1:T(8,128)(2,1)}, u32[]{:S(2)}, u32[]{:S(2)}) collective-permute-start(bf16[4,3,1,8,96,256]{5,4,3,0,2,1:T(8,128)(2,1)S(1)} %pad_maximum_fusion.1), channel_id=1, source_target_pairs={{0,1},{1,2},{2,3},{3,0},{4,5},{5,6},{6,7},{7,4},{8,9},{9,10},{10,1... | collective-permute-start | bytes 14155784 | tf_op jit(solution)/shard_map/ppermute | solution.py:17
  834.9 36.2 %collective-permute-start.12 = (bf16[4,1,1,8,96,256]{5,4,3,0,2,1:T(8,128)(2,1)S(1)}, bf16[4,1,1,8,96,256]{5,4,3,0,2,1:T(8,128)(2,1)S(1)}, u32[]{:S(2)}, u32[]{:S(2)}) collective-permute-start(bf16[4,1,1,8,96,256]{5,4,3,0,2,1:T(8,128)(2,1)S(1)} %fusion.133), channel_id=1, source_target_pairs={{0,4},{4,8},{8,12},{12,0},{1,5},{5,9},{9,13},{13,1},{2,6},{6,10},{... | collective-permute-start | bytes 4718600 | tf_op jit(solution)/shard_map/ppermute | solution.py:17
  834.9 36.2 %collective-permute-start.13 = (bf16[4,1,1,8,96,256]{5,4,3,0,2,1:T(8,128)(2,1)S(1)}, bf16[4,1,1,8,96,256]{5,4,3,0,2,1:T(8,128)(2,1)S(1)}, u32[]{:S(2)}, u32[]{:S(2)}) collective-permute-start(bf16[4,1,1,8,96,256]{5,4,3,0,2,1:T(8,128)(2,1)S(1)} %fusion.136), channel_id=1, source_target_pairs={{4,0},{8,4},{12,8},{0,12},{5,1},{9,5},{13,9},{1,13},{6,2},{10,6},{... | collective-permute-start | bytes 4718600 | tf_op jit(solution)/shard_map/ppermute | solution.py:19
  836.6 39.1 %collective-permute-start.14 = (bf16[4,1,1,8,96,256]{5,4,3,0,2,1:T(8,128)(2,1)S(1)}, bf16[4,1,1,8,96,256]{5,4,3,0,2,1:T(8,128)(2,1)S(1)}, u32[]{:S(2)}, u32[]{:S(2)}) collective-permute-start(bf16[4,1,1,8,96,256]{5,4,3,0,2,1:T(8,128)(2,1)S(1)} %fusion.139), channel_id=1, source_target_pairs={{0,1},{1,2},{2,3},{3,0},{4,5},{5,6},{6,7},{7,4},{8,9},{9,10},{10,1... | collective-permute-start | bytes 4718600 | tf_op jit(solution)/shard_map/ppermute | solution.py:17
  836.6 70.6 %collective-permute-start.15 = (bf16[4,1,1,8,96,256]{5,4,3,0,2,1:T(8,128)(2,1)S(1)}, bf16[4,1,1,8,96,256]{5,4,3,0,2,1:T(8,128)(2,1)}, u32[]{:S(2)}, u32[]{:S(2)}) collective-permute-start(bf16[4,1,1,8,96,256]{5,4,3,0,2,1:T(8,128)(2,1)S(1)} %fusion.142), channel_id=1, source_target_pairs={{1,0},{2,1},{3,2},{0,3},{5,4},{6,5},{7,6},{4,7},{9,8},{10,9},{11,1... | collective-permute-start | bytes 4718600 | tf_op jit(solution)/shard_map/ppermute | solution.py:19
  841.7 65.5 %slice-start.4 = ((bf16[4,1,1,8,96,256]{5,4,3,0,2,1:T(8,128)(2,1)}), bf16[4,1,1,7,96,256]{5,4,3,0,2,1:T(8,128)(2,1)S(1)}, s32[]{:S(2)}) async-start(bf16[4,1,1,8,96,256]{5,4,3,0,2,1:T(8,128)(2,1)} %copy-done.5), calls=%async_computation.6 | async-start | bytes 2752512 | tf_op jit(solution)/shard_map/jit(_roll_static)/slice | solution.py:60
  841.7 65.5 %slice-start.5 = ((bf16[4,1,1,8,96,256]{5,4,3,0,2,1:T(8,128)(2,1)}), bf16[4,1,1,1,96,256]{5,4,3,0,2,1:T(8,128)(2,1)S(1)}, s32[]{:S(2)}) async-start(bf16[4,1,1,8,96,256]{5,4,3,0,2,1:T(8,128)(2,1)} %copy-done.5), calls=%async_computation.7 | async-start | bytes 393216 | tf_op jit(solution)/shard_map/jit(_roll_static)/slice | solution.py:60
  841.8 65.5 %slice-start.6 = ((bf16[4,1,1,8,96,256]{5,4,3,0,2,1:T(8,128)(2,1)}), bf16[4,1,1,7,96,256]{5,4,3,0,2,1:T(8,128)(2,1)S(1)}, s32[]{:S(2)}) async-start(bf16[4,1,1,8,96,256]{5,4,3,0,2,1:T(8,128)(2,1)} %copy-done.6), calls=%async_computation.8 | async-start | bytes 2752512 | tf_op jit(solution)/shard_map/jit(_roll_static)/slice | solution.py:60
  842.0 70.0 %copy-start.3 = (f32[4,1,1,8,96,256]{5,4,3,0,2,1:T(8,128)S(1)}, f32[4,1,1,8,96,256]{5,4,3,0,2,1:T(8,128)}, u32[]{:S(2)}) copy-start(f32[4,1,1,8,96,256]{5,4,3,0,2,1:T(8,128)} %get-tuple-element.96) | copy-start | bytes 9437188
  921.1 161.8 %copy-start.4 = (f32[4,1,1,8,96,256]{5,4,3,0,2,1:T(8,128)S(1)}, f32[4,1,1,8,96,256]{5,4,3,0,2,1:T(8,128)}, u32[]{:S(2)}) copy-start(f32[4,1,1,8,96,256]{5,4,3,0,2,1:T(8,128)} %get-tuple-element.96) | copy-start | bytes 9437188
  (22 other events, 608.0 us)
Sparse Core Ops, SparseCore 0:
  350.8 91.7 all-reduce.6
  918.1 89.0 all-reduce.4
where the time goes:
time: 1100 us
  waiting for transfers between devices  751 us (68%)
  other arithmetic  171 us (16%)
  matrix products  110 us (10%)
  local copies, waits for them, and re-layouts  24.2 us (2%)
  starting transfers between devices  20.3 us (2%)
  between operations  18.5 us (2%)
    ppermute x8, waiting for transfers between devices, with_halo(): lax.ppermute(head, axis, [((i + 1) % count, i) for i in range(count)])  308 us
    ppermute x8, waiting for transfers between devices, with_halo(): lax.ppermute(tail, axis, [(i, (i + 1) % count) for i in range(count)])  264 us
    another operation x21, other arithmetic, solve_spd(): factor = jnp.linalg.cholesky(matrix)  105 us
    psum x1, waiting for transfers between devices, residual_norms(): return lax.psum(gram(residual, residual), ('ta', 'xy'))  91.8 us
    psum x1, waiting for transfers between devices, body(): lax.psum((gram(search, normal_image), gram(residual, normal_image), gram(...  86.1 us
    dot_general x36, matrix products, link_product(): jnp.einsum(einsum_form, link_field, vector, preferred_element_type=jnp.fl...  66.3 us
    another operation x7, other arithmetic, solve_spd(): return jax.scipy.linalg.cho_solve((factor, True), right_side)  62 us
  transfers between devices with their start and end apart: 18, of which 17 were waited for; matrix products, arithmetic and copies ran while one was open for 4% of the time, Pallas kernels for 0%

commit v1 on v0

--- a/solution.py
+++ b/solution.py
@@ -111,12 +111,15 @@
         image_vec = apply_forward(rounded, coarse_links).astype(jnp.bfloat16)
         normal_image = adjoint_products(image_vec, coarse_links)
         curvature, cross_term, image_gram = lax.psum(
-            (
-                gram(search, normal_image),
-                gram(residual, normal_image),
-                gram(normal_image, normal_image),
+            lax.psum(
+                (
+                    gram(search, normal_image),
+                    gram(residual, normal_image),
+                    gram(normal_image, normal_image),
+                ),
+                "xy",
             ),
-            ("ta", "xy"),
+            "ta",
         )
         alpha_step = solve_spd(curvature, energy)
         solution = solution + combine(search, alpha_step)

time: 1100 us -> 1120 us (1.018)
  matrix products: 110 us -> 123 us
    psum x1, waiting for transfers between devices: 91.8 us -> 251 us  [residual_norms(): return lax.psum(gram(residual, residual), ('ta', 'xy'))]
    ppermute x8, waiting for transfers between devices: 264 us -> 162 us  [with_halo(): lax.ppermute(tail, axis, [(i, (i + 1) % count) for i in range(count)])]
    ppermute x8, waiting for transfers between devices: 308 us -> 223 us  [with_halo(): lax.ppermute(head, axis, [((i + 1) % count, i) for i in range(count)])]
    psum x0 -> x2, waiting for transfers between devices: none -> 41.5 us  [body(): lax.psum(lax.psum((gram(search, normal_image), gram(residual, normal_imag...]
    psum x1 -> x2, waiting for transfers between devices: 86.1 us -> 70.9 us  [body(): lax.psum((gram(search, normal_image), gram(residual, normal_image), gram(...]
    another operation x21 -> x20, other arithmetic: 105 us -> 105 us  [solve_spd(): factor = jnp.linalg.cholesky(matrix)]
  transfers between devices with their start and end apart: 18 -> 21, of which waited for: 17 -> 18; matrix products, arithmetic and copies ran while one was open for 4% -> 10% of each run, Pallas kernels for 0% -> 0%
where the time goes in v1:
time: 1120 us; the launch traced here: 1110 us
  waiting for transfers between devices  748 us (67%)
  other arithmetic  173 us (15%)
  matrix products  123 us (11%)
  local copies, waits for them, and re-layouts  25.6 us (2%)
  starting transfers between devices  22.6 us (2%)
  between operations  20.3 us (2%)
    psum x1, waiting for transfers between devices, residual_norms(): return lax.psum(gram(residual, residual), ('ta', 'xy'))  251 us
    ppermute x8, waiting for transfers between devices, with_halo(): lax.ppermute(head, axis, [((i + 1) % count, i) for i in range(count)])  223 us
    ppermute x8, waiting for transfers between devices, with_halo(): lax.ppermute(tail, axis, [(i, (i + 1) % count) for i in range(count)])  162 us
    another operation x20, other arithmetic, solve_spd(): factor = jnp.linalg.cholesky(matrix)  105 us
    dot_general x36, matrix products, link_product(): jnp.einsum(einsum_form, link_field, vector, preferred_element_type=jnp.fl...  76 us
    psum x2, waiting for transfers between devices, body(): lax.psum((gram(search, normal_image), gram(residual, normal_image), gram(...  70.9 us
    another operation x7, other arithmetic, solve_spd(): return jax.scipy.linalg.cho_solve((factor, True), right_side)  60 us
    psum x2, waiting for transfers between devices, body(): lax.psum(lax.psum((gram(search, normal_image), gram(residual, normal_imag...  41.5 us
  transfers between devices with their start and end apart: 21, of which 18 were waited for; matrix products, arithmetic and copies ran while one was open for 10% of the time, Pallas kernels for 0%

profile of v1, /device:TPU:0, one launch (start us, length us, event | category | flops | bytes accessed | tf_op | source)
XLA Modules:
  0.0 1112.7 jit_solution(11169455936561366601)
XLA Ops:
  9.8 35.1 %collective-permute-done = bf16[4,1,1,8,96,256]{5,4,3,0,2,1:T(8,128)(2,1)S(1)} collective-permute-done((bf16[4,1,1,8,96,256]{5,4,3,0,2,1:T(8,128)(2,1)}, bf16[4,1,1,8,96,256]{5,4,3,0,2,1:T(8,128)(2,1)S(1)}, u32[]{:S(2)}, u32[]{:S(2)}) %collective-permute-start) | collective-permute-done | bytes 1572896 | tf_op jit(solution)/shard_map/ppermute | solution.py:19
  69.7 251.1 %all-reduce.9.cloned.1.call-done = f32[256,256]{0,1:T(8,128)} async-done(((f32[256,256]{0,1:T(8,128)}), f32[256,256]{0,1:T(8,128)}) %all-reduce.9.cloned.1.call-update) | async-done | bytes 262160 | tf_op jit(solution)/shard_map/psum | solution.py:101
  323.6 11.7 %cholesky.206 = f32[128,128]{1,0:T(8,128)S(1)} custom-call(f32[128,128]{1,0:T(8,128)S(1)} %cholesky.273), custom_call_target="Cholesky" | custom-call | tf_op jit(solution)/shard_map/jit(cholesky)/cholesky | solution.py:96
  335.4 10.4 custom-call.19
  348.7 12.9 %cholesky.223 = f32[128,128]{1,0:T(8,128)S(1)} custom-call(f32[128,128]{1,0:T(8,128)} %convolution_subtract_fusion.7), custom_call_target="Cholesky" | custom-call | tf_op jit(solution)/shard_map/jit(cholesky)/cholesky | solution.py:96
  394.0 26.3 %collective-permute-done.4 = bf16[4,1,1,8,96,256]{5,4,3,0,2,1:T(8,128)(2,1)S(1)} collective-permute-done((bf16[4,1,1,8,96,256]{5,4,3,0,2,1:T(8,128)(2,1)S(1)}, bf16[4,1,1,8,96,256]{5,4,3,0,2,1:T(8,128)(2,1)S(1)}, u32[]{:S(2)}, u32[]{:S(2)}) %collective-permute-start.4) | collective-permute-done | bytes 1572896 | tf_op jit(solution)/shard_map/ppermute | solution.py:17
  425.4 31.9 %collective-permute-done.7 = bf16[4,1,1,8,96,256]{5,4,3,0,2,1:T(8,128)(2,1)S(1)} collective-permute-done((bf16[4,1,1,8,96,256]{5,4,3,0,2,1:T(8,128)(2,1)S(1)}, bf16[4,1,1,8,96,256]{5,4,3,0,2,1:T(8,128)(2,1)S(1)}, u32[]{:S(2)}, u32[]{:S(2)}) %collective-permute-start.7) | collective-permute-done | bytes 1572896 | tf_op jit(solution)/shard_map/ppermute | solution.py:19
  474.0 36.9 %all-reduce.15.cloned.1.call-done = (f32[256,256]{0,1:T(8,128)}, f32[256,256]{1,0:T(8,128)}) async-done(((f32[256,256]{0,1:T(8,128)}, f32[256,256]{1,0:T(8,128)}), (f32[256,256]{0,1:T(8,128)}, f32[256,256]{1,0:T(8,128)})) %all-reduce.15.cloned.1.call-update) | async-done | bytes 524304 | tf_op jit(solution)/shard_map/psum | solution.py:114
  515.4 20.3 %custom-call.20 = f32[2,128,128]{1,2,0:T(8,128)} custom-call(f32[2,128,128]{2,1,0:T(8,128)S(1)} %get-tuple-element.28), custom_call_target="InvertDiagBlocksLowerTriangular" | custom-call | tf_op jit(solution)/shard_map/jit(_cho_solve)/triangular_solve | solution.py:97
  535.7 10.7 all-reduce.17.cloned.1.call-done
  548.6 11.7 %cholesky.172 = f32[128,128]{1,0:T(8,128)S(1)} custom-call(f32[128,128]{1,0:T(8,128)S(1)} %cholesky.270), custom_call_target="Cholesky" | custom-call | tf_op jit(solution)/shard_map/jit(cholesky)/cholesky | solution.py:96
  560.3 9.8 custom-call.17
  570.6 11.7 %cholesky.189 = f32[128,128]{1,0:T(8,128)S(1)} custom-call(f32[128,128]{1,0:T(8,128)S(1)} %convolution_subtract_fusion.8), custom_call_target="Cholesky" | custom-call | tf_op jit(solution)/shard_map/jit(cholesky)/cholesky | solution.py:96
  589.3 19.9 %custom-call.18 = f32[2,128,128]{1,2,0:T(8,128)S(1)} custom-call(f32[2,128,128]{2,1,0:T(8,128)S(1)} %get-tuple-element.27), custom_call_target="InvertDiagBlocksLowerTriangular" | custom-call | tf_op jit(solution)/shard_map/jit(_cho_solve)/triangular_solve | solution.py:97
  624.1 34.1 %collective-permute-done.8 = bf16[4,1,1,8,96,256]{5,4,3,0,2,1:T(8,128)(2,1)S(1)} collective-permute-done((bf16[4,1,1,8,96,256]{5,4,3,0,2,1:T(8,128)(2,1)S(1)}, bf16[4,1,1,8,96,256]{5,4,3,0,2,1:T(8,128)(2,1)S(1)}, u32[]{:S(2)}, u32[]{:S(2)}) %collective-permute-start.8) | collective-permute-done | bytes 1572896 | tf_op jit(solution)/shard_map/ppermute | solution.py:19
  678.4 86.9 %collective-permute-done.10 = bf16[4,3,1,8,96,256]{5,4,3,0,2,1:T(8,128)(2,1)S(1)} collective-permute-done((bf16[4,3,1,8,96,256]{5,4,3,0,2,1:T(8,128)(2,1)S(1)}, bf16[4,3,1,8,96,256]{5,4,3,0,2,1:T(8,128)(2,1)S(1)}, u32[]{:S(2)}, u32[]{:S(2)}) %collective-permute-start.10) | collective-permute-done | bytes 4718624 | tf_op jit(solution)/shard_map/ppermute | solution.py:19
  767.5 98.0 %collective-permute-done.11 = bf16[4,3,1,8,96,256]{5,4,3,0,2,1:T(8,128)(2,1)} collective-permute-done((bf16[4,3,1,8,96,256]{5,4,3,0,2,1:T(8,128)(2,1)S(1)}, bf16[4,3,1,8,96,256]{5,4,3,0,2,1:T(8,128)(2,1)}, u32[]{:S(2)}, u32[]{:S(2)}) %collective-permute-start.11) | collective-permute-done | bytes 4718624 | tf_op jit(solution)/shard_map/ppermute | solution.py:17
  887.3 26.7 %collective-permute-done.12 = bf16[4,1,1,8,96,256]{5,4,3,0,2,1:T(8,128)(2,1)S(1)} collective-permute-done((bf16[4,1,1,8,96,256]{5,4,3,0,2,1:T(8,128)(2,1)S(1)}, bf16[4,1,1,8,96,256]{5,4,3,0,2,1:T(8,128)(2,1)S(1)}, u32[]{:S(2)}, u32[]{:S(2)}) %collective-permute-start.12) | collective-permute-done | bytes 1572896 | tf_op jit(solution)/shard_map/ppermute | solution.py:17
  922.0 32.1 %collective-permute-done.15 = bf16[4,1,1,8,96,256]{5,4,3,0,2,1:T(8,128)(2,1)} collective-permute-done((bf16[4,1,1,8,96,256]{5,4,3,0,2,1:T(8,128)(2,1)S(1)}, bf16[4,1,1,8,96,256]{5,4,3,0,2,1:T(8,128)(2,1)}, u32[]{:S(2)}, u32[]{:S(2)}) %collective-permute-start.15) | collective-permute-done | bytes 1572896 | tf_op jit(solution)/shard_map/ppermute | solution.py:19
  965.1 34.0 %all-reduce.11.cloned.1.call-done = f32[256,256]{0,1:T(8,128)} async-done(((f32[256,256]{0,1:T(8,128)}), f32[256,256]{0,1:T(8,128)}) %all-reduce.11.cloned.1.call-update) | async-done | bytes 262160 | tf_op jit(solution)/shard_map/psum | solution.py:114
  1002.2 30.8 %all-reduce.13.cloned.1.call-done = f32[256,256]{0,1:T(8,128)} async-done(((f32[256,256]{0,1:T(8,128)}), f32[256,256]{0,1:T(8,128)}) %all-reduce.13.cloned.1.call-update) | async-done | bytes 262160 | tf_op jit(solution)/shard_map/psum | solution.py:113
  1035.0 11.7 %cholesky.240 = f32[128,128]{1,0:T(8,128)S(1)} custom-call(f32[128,128]{1,0:T(8,128)S(1)} %cholesky.276), custom_call_target="Cholesky" | custom-call | tf_op jit(solution)/shard_map/jit(cholesky)/cholesky | solution.py:96
  1057.1 11.7 %cholesky.257 = f32[128,128]{1,0:T(8,128)S(1)} custom-call(f32[128,128]{1,0:T(8,128)S(1)} %convolution_subtract_fusion.6), custom_call_target="Cholesky" | custom-call | tf_op jit(solution)/shard_map/jit(cholesky)/cholesky | solution.py:96
  1075.9 19.7 %custom-call.22 = f32[2,128,128]{1,2,0:T(8,128)S(1)} custom-call(f32[2,128,128]{2,1,0:T(8,128)S(1)} %get-tuple-element.29), custom_call_target="InvertDiagBlocksLowerTriangular" | custom-call | tf_op jit(solution)/shard_map/jit(_cho_solve)/triangular_solve | solution.py:97
  (239 shorter events, 218.3 us)
Async XLA Ops:
  7.4 313.5 %all-reduce.9.cloned.1.call-start = ((), (), s32[]{:S(2)}) async-start(), calls=%async_computation | async-start | bytes 524288 | tf_op jit(solution)/shard_map/psum | solution.py:101
  7.4 37.5 %collective-permute-start = (bf16[4,1,1,8,96,256]{5,4,3,0,2,1:T(8,128)(2,1)}, bf16[4,1,1,8,96,256]{5,4,3,0,2,1:T(8,128)(2,1)S(1)}, u32[]{:S(2)}, u32[]{:S(2)}) collective-permute-start(bf16[4,1,1,8,96,256]{5,4,3,0,2,1:T(8,128)(2,1)} %bitcast.587), channel_id=1, source_target_pairs={{4,0},{8,4},{12,8},{0,12},{5,1},{9,5},{13,9},{1,13},{6,2},{10,6},{... | collective-permute-start | bytes 4718600 | tf_op jit(solution)/shard_map/ppermute | solution.py:19
  9.8 36.1 %collective-permute-start.1 = (bf16[4,1,1,8,96,256]{5,4,3,0,2,1:T(8,128)(2,1)}, bf16[4,1,1,8,96,256]{5,4,3,0,2,1:T(8,128)(2,1)S(1)}, u32[]{:S(2)}, u32[]{:S(2)}) collective-permute-start(bf16[4,1,1,8,96,256]{5,4,3,0,2,1:T(8,128)(2,1)} %bitcast.588), channel_id=1, source_target_pairs={{0,4},{4,8},{8,12},{12,0},{1,5},{5,9},{9,13},{13,1},{2,6},{6,10},{... | collective-permute-start | bytes 4718600 | tf_op jit(solution)/shard_map/ppermute | solution.py:17
  50.0 319.2 %collective-permute-start.2 = (bf16[4,3,1,8,96,256]{5,4,3,0,2,1:T(8,128)(2,1)}, bf16[4,3,1,8,96,256]{5,4,3,0,2,1:T(8,128)(2,1)}, u32[]{:S(2)}, u32[]{:S(2)}) collective-permute-start(bf16[4,3,1,8,96,256]{5,4,3,0,2,1:T(8,128)(2,1)} %pad_maximum_fusion), channel_id=1, source_target_pairs={{1,0},{2,1},{3,2},{0,3},{5,4},{6,5},{7,6},{4,7},{9,8},{10,9},{11,1... | collective-permute-start | bytes 14155784 | tf_op jit(solution)/shard_map/ppermute | solution.py:19
  55.1 455.9 %all-reduce.15.cloned.1.call-start = ((), (), s32[]{:S(2)}) async-start(), calls=%async_computation.3 | async-start | bytes 1048576 | tf_op jit(solution)/shard_map/psum | solution.py:114
  55.1 318.0 %collective-permute-start.3 = (bf16[4,3,1,8,96,256]{5,4,3,0,2,1:T(8,128)(2,1)}, bf16[4,3,1,8,96,256]{5,4,3,0,2,1:T(8,128)(2,1)}, u32[]{:S(2)}, u32[]{:S(2)}) collective-permute-start(bf16[4,3,1,8,96,256]{5,4,3,0,2,1:T(8,128)(2,1)} %pad_maximum_fusion), channel_id=1, source_target_pairs={{0,1},{1,2},{2,3},{3,0},{4,5},{5,6},{6,7},{7,4},{8,9},{9,10},{10,1... | collective-permute-start | bytes 14155784 | tf_op jit(solution)/shard_map/ppermute | solution.py:17
  384.5 35.9 %collective-permute-start.4 = (bf16[4,1,1,8,96,256]{5,4,3,0,2,1:T(8,128)(2,1)S(1)}, bf16[4,1,1,8,96,256]{5,4,3,0,2,1:T(8,128)(2,1)S(1)}, u32[]{:S(2)}, u32[]{:S(2)}) collective-permute-start(bf16[4,1,1,8,96,256]{5,4,3,0,2,1:T(8,128)(2,1)S(1)} %fusion.109), channel_id=1, source_target_pairs={{0,4},{4,8},{8,12},{12,0},{1,5},{5,9},{9,13},{13,1},{2,6},{6,10},{... | collective-permute-start | bytes 4718600 | tf_op jit(solution)/shard_map/ppermute | solution.py:17
  385.0 35.4 %collective-permute-start.5 = (bf16[4,1,1,8,96,256]{5,4,3,0,2,1:T(8,128)(2,1)S(1)}, bf16[4,1,1,8,96,256]{5,4,3,0,2,1:T(8,128)(2,1)S(1)}, u32[]{:S(2)}, u32[]{:S(2)}) collective-permute-start(bf16[4,1,1,8,96,256]{5,4,3,0,2,1:T(8,128)(2,1)S(1)} %fusion.112), channel_id=1, source_target_pairs={{4,0},{8,4},{12,8},{0,12},{5,1},{9,5},{13,9},{1,13},{6,2},{10,6},{... | collective-permute-start | bytes 4718600 | tf_op jit(solution)/shard_map/ppermute | solution.py:19
  386.3 39.1 %collective-permute-start.6 = (bf16[4,1,1,8,96,256]{5,4,3,0,2,1:T(8,128)(2,1)S(1)}, bf16[4,1,1,8,96,256]{5,4,3,0,2,1:T(8,128)(2,1)S(1)}, u32[]{:S(2)}, u32[]{:S(2)}) collective-permute-start(bf16[4,1,1,8,96,256]{5,4,3,0,2,1:T(8,128)(2,1)S(1)} %fusion.115), channel_id=1, source_target_pairs={{0,1},{1,2},{2,3},{3,0},{4,5},{5,6},{6,7},{7,4},{8,9},{9,10},{10,1... | collective-permute-start | bytes 4718600 | tf_op jit(solution)/shard_map/ppermute | solution.py:17
  389.2 68.1 %collective-permute-start.7 = (bf16[4,1,1,8,96,256]{5,4,3,0,2,1:T(8,128)(2,1)S(1)}, bf16[4,1,1,8,96,256]{5,4,3,0,2,1:T(8,128)(2,1)S(1)}, u32[]{:S(2)}, u32[]{:S(2)}) collective-permute-start(bf16[4,1,1,8,96,256]{5,4,3,0,2,1:T(8,128)(2,1)S(1)} %fusion.118), channel_id=1, source_target_pairs={{1,0},{2,1},{3,2},{0,3},{5,4},{6,5},{7,6},{4,7},{9,8},{10,9},{11,1... | collective-permute-start | bytes 4718600 | tf_op jit(solution)/shard_map/ppermute | solution.py:19
  471.9 137.3 %copy-start.12 = (f32[256,256]{0,1:T(8,128)S(1)}, f32[256,256]{0,1:T(8,128)}, u32[]{:S(2)}) copy-start(f32[256,256]{0,1:T(8,128)} %all-reduce.9.cloned.1.call-done) | copy-start | bytes 786436
  471.9 74.5 %all-reduce.17.cloned.1.call-start = ((), (), s32[]{:S(2)}) async-start(), calls=%async_computation.4 | async-start | bytes 1048576 | tf_op jit(solution)/shard_map/psum | solution.py:113
  511.0 488.1 %all-reduce.11.cloned.1.call-start = ((), (), s32[]{:S(2)}) async-start(), calls=%async_computation.1 | async-start | bytes 524288 | tf_op jit(solution)/shard_map/psum | solution.py:114
  623.5 335.3 %copy-start.4 = (f32[4,1,1,8,96,256]{5,4,3,0,2,1:T(8,128)}, f32[4,1,1,8,96,256]{5,4,3,0,2,1:T(8,128)S(1)}, u32[]{:S(2)}) copy-start(f32[4,1,1,8,96,256]{5,4,3,0,2,1:T(8,128)S(1)} %get-tuple-element.97) | copy-start | bytes 9437188
  623.5 34.7 %collective-permute-start.8 = (bf16[4,1,1,8,96,256]{5,4,3,0,2,1:T(8,128)(2,1)S(1)}, bf16[4,1,1,8,96,256]{5,4,3,0,2,1:T(8,128)(2,1)S(1)}, u32[]{:S(2)}, u32[]{:S(2)}) collective-permute-start(bf16[4,1,1,8,96,256]{5,4,3,0,2,1:T(8,128)(2,1)S(1)} %get-tuple-element.96), channel_id=1, source_target_pairs={{4,0},{8,4},{12,8},{0,12},{5,1},{9,5},{13,9},{1,13},{6,2},{10,6},{... | collective-permute-start | bytes 4718600 | tf_op jit(solution)/shard_map/ppermute | solution.py:19
  623.6 35.3 %collective-permute-start.9 = (bf16[4,1,1,8,96,256]{5,4,3,0,2,1:T(8,128)(2,1)S(1)}, bf16[4,1,1,8,96,256]{5,4,3,0,2,1:T(8,128)(2,1)S(1)}, u32[]{:S(2)}, u32[]{:S(2)}) collective-permute-start(bf16[4,1,1,8,96,256]{5,4,3,0,2,1:T(8,128)(2,1)S(1)} %get-tuple-element.96), channel_id=1, source_target_pairs={{0,4},{4,8},{8,12},{12,0},{1,5},{5,9},{9,13},{13,1},{2,6},{6,10},{... | collective-permute-start | bytes 4718600 | tf_op jit(solution)/shard_map/ppermute | solution.py:17
  659.5 105.9 %collective-permute-start.10 = (bf16[4,3,1,8,96,256]{5,4,3,0,2,1:T(8,128)(2,1)S(1)}, bf16[4,3,1,8,96,256]{5,4,3,0,2,1:T(8,128)(2,1)S(1)}, u32[]{:S(2)}, u32[]{:S(2)}) collective-permute-start(bf16[4,3,1,8,96,256]{5,4,3,0,2,1:T(8,128)(2,1)S(1)} %pad_maximum_fusion.1), channel_id=1, source_target_pairs={{1,0},{2,1},{3,2},{0,3},{5,4},{6,5},{7,6},{4,7},{9,8},{10,9},{11,1... | collective-permute-start | bytes 14155784 | tf_op jit(solution)/shard_map/ppermute | solution.py:19
  663.1 202.4 %collective-permute-start.11 = (bf16[4,3,1,8,96,256]{5,4,3,0,2,1:T(8,128)(2,1)S(1)}, bf16[4,3,1,8,96,256]{5,4,3,0,2,1:T(8,128)(2,1)}, u32[]{:S(2)}, u32[]{:S(2)}) collective-permute-start(bf16[4,3,1,8,96,256]{5,4,3,0,2,1:T(8,128)(2,1)S(1)} %pad_maximum_fusion.1), channel_id=1, source_target_pairs={{0,1},{1,2},{2,3},{3,0},{4,5},{5,6},{6,7},{7,4},{8,9},{9,10},{10,1... | collective-permute-start | bytes 14155784 | tf_op jit(solution)/shard_map/ppermute | solution.py:17
  880.0 34.0 %collective-permute-start.12 = (bf16[4,1,1,8,96,256]{5,4,3,0,2,1:T(8,128)(2,1)S(1)}, bf16[4,1,1,8,96,256]{5,4,3,0,2,1:T(8,128)(2,1)S(1)}, u32[]{:S(2)}, u32[]{:S(2)}) collective-permute-start(bf16[4,1,1,8,96,256]{5,4,3,0,2,1:T(8,128)(2,1)S(1)} %fusion.133), channel_id=1, source_target_pairs={{0,4},{4,8},{8,12},{12,0},{1,5},{5,9},{9,13},{13,1},{2,6},{6,10},{... | collective-permute-start | bytes 4718600 | tf_op jit(solution)/shard_map/ppermute | solution.py:17
  880.0 36.4 %collective-permute-start.13 = (bf16[4,1,1,8,96,256]{5,4,3,0,2,1:T(8,128)(2,1)S(1)}, bf16[4,1,1,8,96,256]{5,4,3,0,2,1:T(8,128)(2,1)S(1)}, u32[]{:S(2)}, u32[]{:S(2)}) collective-permute-start(bf16[4,1,1,8,96,256]{5,4,3,0,2,1:T(8,128)(2,1)S(1)} %fusion.136), channel_id=1, source_target_pairs={{4,0},{8,4},{12,8},{0,12},{5,1},{9,5},{13,9},{1,13},{6,2},{10,6},{... | collective-permute-start | bytes 4718600 | tf_op jit(solution)/shard_map/ppermute | solution.py:19
  881.8 39.1 %collective-permute-start.14 = (bf16[4,1,1,8,96,256]{5,4,3,0,2,1:T(8,128)(2,1)S(1)}, bf16[4,1,1,8,96,256]{5,4,3,0,2,1:T(8,128)(2,1)S(1)}, u32[]{:S(2)}, u32[]{:S(2)}) collective-permute-start(bf16[4,1,1,8,96,256]{5,4,3,0,2,1:T(8,128)(2,1)S(1)} %fusion.139), channel_id=1, source_target_pairs={{0,1},{1,2},{2,3},{3,0},{4,5},{5,6},{6,7},{7,4},{8,9},{9,10},{10,1... | collective-permute-start | bytes 4718600 | tf_op jit(solution)/shard_map/ppermute | solution.py:17
  883.3 70.8 %collective-permute-start.15 = (bf16[4,1,1,8,96,256]{5,4,3,0,2,1:T(8,128)(2,1)S(1)}, bf16[4,1,1,8,96,256]{5,4,3,0,2,1:T(8,128)(2,1)}, u32[]{:S(2)}, u32[]{:S(2)}) collective-permute-start(bf16[4,1,1,8,96,256]{5,4,3,0,2,1:T(8,128)(2,1)S(1)} %fusion.142), channel_id=1, source_target_pairs={{1,0},{2,1},{3,2},{0,3},{5,4},{6,5},{7,6},{4,7},{9,8},{10,9},{11,1... | collective-permute-start | bytes 4718600 | tf_op jit(solution)/shard_map/ppermute | solution.py:19
  887.0 67.1 %slice-start.4 = ((bf16[4,1,1,8,96,256]{5,4,3,0,2,1:T(8,128)(2,1)}), bf16[4,1,1,7,96,256]{5,4,3,0,2,1:T(8,128)(2,1)S(1)}, s32[]{:S(2)}) async-start(bf16[4,1,1,8,96,256]{5,4,3,0,2,1:T(8,128)(2,1)} %copy-done.8), calls=%async_computation.9 | async-start | bytes 2752512 | tf_op jit(solution)/shard_map/jit(_roll_static)/slice | solution.py:60
  964.8 68.1 %all-reduce.13.cloned.1.call-start = ((), (), s32[]{:S(2)}) async-start(), calls=%async_computation.2 | async-start | bytes 524288 | tf_op jit(solution)/shard_map/psum | solution.py:113
  (28 other events, 720.1 us)
Sparse Core Ops, SparseCore 0:
  55.2 265.6 all-reduce.8
Sparse Core Ops, SparseCore 1:
  472.0 38.9 all-reduce.14
  513.2 33.1 all-reduce.16
  964.9 34.1 all-reduce.10
  1001.4 31.5 all-reduce.12
